TPU v7x, 32 devices: a whole 2x2x4 slice. The times are simulated.
32 devices in a mesh: lat: 2 (over core), lon: 16 (over z, y, x).
Axes of the slice: x: 2, y: 2, z: 4, core: 2. Of those that a mesh axis runs over, the one named last changes fastest.
Arguments:
- stream: bfloat16 [32, 256, 256], P('lat', 'lon'), may hold values from -6 to 6
- gains: float32 [2, 2, 256], replicated, may hold values from 0.5 to 1.5
- w_qkv: bfloat16 [2, 256, 768], replicated, may hold values from -8 to 8
- table: float32 [2, 4, 13, 7], replicated, may hold values from -4 to 4
- w_out: bfloat16 [2, 256, 256], replicated, may hold values from -0.375 to 0.375
- w_up: bfloat16 [2, 256, 768], replicated, may hold values from -0.375 to 0.375
- kernel: float32 [2, 3, 3, 768], replicated, may hold values from -2 to 2
- w_down: bfloat16 [2, 768, 256], replicated, may hold values from -0.21875 to 0.21875
Outputs:
- result: bfloat16 [32, 256, 256], P('lat', 'lon')
All inputs are finite; a program needn't handle non-finite values.
Results may differ from a plain program's by a relative error of at most 0.013.
Values may be sent and summed in bfloat16 or wider, within the bound.
A program may use at most 64 MiB of HBM per device.

v0:
```python
import functools

import jax
import jax.numpy as jnp
from jax import lax
from jax.experimental import pallas as pl
from jax.experimental.pallas import tpu as pltpu
from jax.sharding import PartitionSpec as P

WINDOW = 7
REACH = 3
GROUP = 4
F32 = jnp.float32
BF16 = jnp.bfloat16

LEFT, RIGHT, TOP, BOTTOM, TOP_L, TOP_R, BOT_L, BOT_R = range(8)
STEPS = ((0, 1), (0, -1), (1, 0), (-1, 0), (1, 1), (1, -1), (-1, 1), (-1, -1))


def iota(shape, dim):
    return lax.broadcasted_iota(jnp.int32, shape, dim)


def hot(cond):
    return jnp.where(cond, 1.0, 0.0).astype(BF16)


def dot(a, b):
    return jnp.dot(a, b, preferred_element_type=F32)


def normed(wide, gain):
    scale = lax.rsqrt(jnp.mean(wide * wide, axis=-1, keepdims=True) + 1e-06)
    return (wide * scale * gain).astype(BF16)


def kernel(
    n_lat, n_lon, x_ref, gains_ref, table_ref, conv_ref, wqkv_hbm, wout_hbm, wup_hbm, wdown_hbm,
    out_ref, wqkv, wout, wup, wdown, kvb, left, right, edge, lifted, ledge, halo, lpad, pre, flat,
    bias, attn, w_sem, send_sem, recv_sem,
):
    layers = wqkv.shape[0]
    tokens, width = x_ref.shape
    cols = 16
    heads = table_ref.shape[0] // layers
    hid = wup.shape[2]
    lat = lax.axis_index("lat")
    lon = lax.axis_index("lon")
    has_up = lat > 0
    has_down = lat < n_lat - 1
    total_rows = n_lat * (tokens // cols)
    first_row = lat * (tokens // cols)

    loads = {}
    for n in range(layers):
        pairs = ((wqkv_hbm, wqkv), (wout_hbm, wout), (wup_hbm, wup), (wdown_hbm, wdown))
        for k, (src, dst) in enumerate(pairs):
            loads[n, k] = pltpu.make_async_copy(src.at[n], dst.at[n], w_sem.at[n, k])
            loads[n, k].start()

    def target(step):
        return {"lat": lat + step[0], "lon": lax.rem(lon + step[1] + n_lon, n_lon)}

    def when_to(step, go):
        if step[0] == 0:
            go()
        else:
            pl.when(has_down if step[0] > 0 else has_up)(go)

    def when_from(step, go):
        when_to((-step[0], -step[1]), go)

    barrier = pltpu.get_barrier_semaphore()
    for step in STEPS:
        when_to(
            step,
            lambda step=step: pl.semaphore_signal(
                barrier, inc=1, device_id=target(step), device_id_type=pl.DeviceIdType.MESH
            ),
        )

    def messages(n, which):
        if which == 0:
            kv, lo, ro, ed = kvb.at[n], left.at[n], right.at[n], edge.at[n]
            return (
                (ed.at[pl.ds(64, 64)], lo.at[pl.ds(16, 64)]),
                (ed.at[pl.ds(0, 64)], ro.at[pl.ds(16, 64)]),
                (kv.at[pl.ds(256, 48)], kv.at[pl.ds(0, 48)]),
                (kv.at[pl.ds(48, 48)], kv.at[pl.ds(304, 48)]),
                (ed.at[pl.ds(112, 16)], lo.at[pl.ds(0, 16)]),
                (ed.at[pl.ds(48, 16)], ro.at[pl.ds(0, 16)]),
                (ed.at[pl.ds(64, 16)], lo.at[pl.ds(80, 16)]),
                (ed.at[pl.ds(0, 16)], ro.at[pl.ds(80, 16)]),
            )
        low, high = lifted.at[n, pl.ds(0, 16)], lifted.at[n, pl.ds(240, 16)]
        sources = (
            ledge.at[n, pl.ds(16, 16)], ledge.at[n, pl.ds(0, 16)], high, low, high, high, low, low,
        )
        return tuple((src, halo.at[n, slot]) for slot, src in enumerate(sources))

    def remote(n, which, slot):
        src, dst = messages(n, which)[slot]
        return pltpu.make_async_remote_copy(
            src_ref=src,
            dst_ref=dst,
            send_sem=send_sem.at[2 * n + which, slot],
            recv_sem=recv_sem.at[2 * n + which, slot],
            device_id=target(STEPS[slot]),
            device_id_type=pl.DeviceIdType.MESH,
        )

    def send(n, which):
        for slot, step in enumerate(STEPS):
            when_to(step, lambda slot=slot: remote(n, which, slot).start())

    def receive(n, which):
        for slot, step in enumerate(STEPS):
            when_from(step, lambda slot=slot: remote(n, which, slot).wait_recv())

    @pl.when(jnp.logical_not(has_up))
    def _():
        for n in range(layers):
            kvb[n, 0:48] = jnp.zeros((48, 2 * width), BF16)
            left[n, 0:16] = jnp.zeros((16, 2 * width), BF16)
            right[n, 0:16] = jnp.zeros((16, 2 * width), BF16)
            for slot in (TOP, TOP_L, TOP_R):
                halo[n, slot] = jnp.zeros((16, hid), BF16)

    @pl.when(jnp.logical_not(has_down))
    def _():
        for n in range(layers):
            kvb[n, 304:352] = jnp.zeros((48, 2 * width), BF16)
            left[n, 80:96] = jnp.zeros((16, 2 * width), BF16)
            right[n, 80:96] = jnp.zeros((16, 2 * width), BF16)
            for slot in (BOTTOM, BOT_L, BOT_R):
                halo[n, slot] = jnp.zeros((16, hid), BF16)

    lpad[0:16] = jnp.zeros((16, hid), F32)
    lpad[272:288] = jnp.zeros((16, hid), F32)

    m, t = iota((128, tokens), 0), iota((128, tokens), 1)
    pick_kv = hot(t == ((m & 63) >> 2) * cols + (m & 3) + jnp.where(m >= 64, cols - 4, 0))
    m, t = iota((32, tokens), 0), iota((32, tokens), 1)
    pick_lift = hot(t == (m & 15) * cols + jnp.where(m >= 16, cols - 1, 0))
    t, k = iota((tokens, 64), 0), iota((tokens, 64), 1)
    place = hot(((k & 15) == (t >> 4)) & ((t & 15) == jnp.where(k < 32, 0, cols - 1)))
    head_of = iota((1, width), 1) >> 6
    head_hot = [hot(head_of == h) for h in range(heads)]

    def build_bias():
        flat[...] = jnp.zeros_like(flat)
        for a in range(2 * WINDOW - 1):
            row = table_ref[:, a, :]
            flat[0, :, 16 * a : 16 * a + 7] = row
            flat[1, :, 4 * a : 4 * a + 3] = row[:, 0:3]
            flat[2, :, 4 * a : 4 * a + 4] = row[:, 3:7]
        x = iota((16, 256), 1)
        j = iota((16, 256), 0)
        own = x < 160
        on_left = x < 208
        y = jnp.where(on_left, x - 160, x - 208)
        p = jnp.where(own, x >> 4, (y >> 2) - 1)
        c = jnp.where(own, x & 15, jnp.where(on_left, (y & 3) - 4, (y & 3) + cols))
        col_ok = (c - j >= -REACH) & (c - j <= REACH)
        for i in range(GROUP):
            oks = []
            for group in (0, 1, 3):
                g = first_row + GROUP * group + i
                start = jnp.clip(g - REACH, 0, total_rows - WINDOW)
                r = first_row + GROUP * group - REACH + p
                oks.append(col_ok & (r >= start) & (r < start + WINDOW))
            for n in range(layers):
                for h in range(heads):
                    row = n * heads + h

                    def turned(which, shift):
                        base = pltpu.roll(flat[which, row : row + 1, :], shift % 256, 1)
                        base = jnp.broadcast_to(base, (16, 256))
                        return pltpu.roll(base, 0, 1, stride=1, stride_axis=0)

                    value = jnp.where(
                        own,
                        turned(0, 16 * i - 51),
                        jnp.where(
                            on_left, turned(1, 160 + 4 * i - 7), turned(2, 208 + 4 * i - 24)
                        ),
                    )
                    at = h * 64 + i * 16
                    for var in range(3):
                        bias[n, var, at : at + 16, :] = jnp.where(oks[var], value, -1000000000.0)

    wide = x_ref[...].astype(F32)
    for n in range(layers):
        norm = normed(wide, gains_ref[n, 0:1, :])
        loads[n, 0].wait()
        kv = dot(norm, wqkv[n, :, width:]).astype(BF16)
        kvb[n, 48:304] = kv
        edge[n] = dot(pick_kv, kv).astype(BF16)
        if n == 0:
            count = 2 + jnp.where(has_up, 3, 0) + jnp.where(has_down, 3, 0)
            pl.semaphore_wait(barrier, count)
        send(n, 0)
        query = (dot(norm, wqkv[n, :, :width]).astype(BF16) * (width // heads) ** (-0.5)).astype(BF16)
        if n == 0:
            build_bias()
        receive(n, 0)
        for group in range(4):
            parts = [
                kvb[n, 64 * group : 64 * group + 160, :],
                left[n, 16 * group : 16 * group + 48, :],
                right[n, 16 * group : 16 * group + 48, :],
            ]
            near = jnp.concatenate(parts, axis=0)
            q = query[64 * group : 64 * group + 64, :]
            stacked = jnp.concatenate([q * head_hot[h] for h in range(heads)], axis=0)
            scores = lax.dot_general(
                stacked, near[:, :width], (((1,), (1,)), ((), ())), preferred_element_type=F32
            )
            scores = scores + bias[n, (0, 1, 1, 2)[group]]
            raised = jnp.exp(scores - jnp.max(scores, axis=-1, keepdims=True))
            weights = (raised * (1.0 / jnp.sum(raised, axis=-1, keepdims=True))).astype(BF16)
            mixed = dot(weights, near[:, width:])
            total = jnp.where(head_of == 0, mixed[0:64], 0.0)
            for h in range(1, heads):
                total = jnp.where(head_of == h, mixed[64 * h : 64 * h + 64], total)
            attn[64 * group : 64 * group + 64, :] = total.astype(BF16)
        loads[n, 1].wait()
        after = wide + dot(attn[...], wout[n])
        norm = normed(after, gains_ref[n, 1:2, :])
        loads[n, 2].wait()
        lift = dot(norm, wup[n]).astype(BF16)
        lifted[n] = lift
        ledge[n] = dot(pick_lift, lift).astype(BF16)
        send(n, 1)
        lpad[16:272] = lift.astype(F32)
        col = iota((tokens, 128), 0) & 15
        for ch in range(hid // 128):
            at = slice(128 * ch, 128 * ch + 128)
            above, here, below = lpad[0:256, at], lpad[16:272, at], lpad[32:288, at]

            def column(b):
                return (
                    conv_ref[n, 0, b : b + 1, at] * above
                    + conv_ref[n, 1, b : b + 1, at] * here
                    + conv_ref[n, 2, b : b + 1, at] * below
                )

            pre[:, at] = (
                column(1)
                + jnp.where(col > 0, pltpu.roll(column(0), 1, 0), 0.0)
                + jnp.where(col < cols - 1, pltpu.roll(column(2), tokens - 1, 0), 0.0)
            )
        receive(n, 1)
        line = iota((16, hid), 0)
        got = [halo[n, slot].astype(F32) for slot in range(8)]

        def tap(a, b):
            return conv_ref[n, a, b : b + 1, :]

        def row_part(a, middle, at_left, at_right):
            back = jnp.where(line == 0, pltpu.roll(at_left, 1, 0), pltpu.roll(middle, 1, 0))
            ahead = jnp.where(line == 15, pltpu.roll(at_right, 15, 0), pltpu.roll(middle, 15, 0))
            return tap(a, 0) * back + tap(a, 1) * middle + tap(a, 2) * ahead

        def col_part(b, values):
            up = jnp.where(line == 0, 0.0, pltpu.roll(values, 1, 0))
            down = jnp.where(line == 15, 0.0, pltpu.roll(values, 15, 0))
            return tap(0, b) * up + tap(1, b) * values + tap(2, b) * down

        pieces = []
        for part in (col_part(0, got[LEFT]), col_part(2, got[RIGHT])):
            high = part.astype(BF16)
            pieces += [high, (part - high.astype(F32)).astype(BF16)]
        pre[0:16] += row_part(0, got[TOP], got[TOP_L], got[TOP_R])
        pre[240:256] += row_part(2, got[BOTTOM], got[BOT_L], got[BOT_R])
        whole = pre[...] + dot(place, jnp.concatenate(pieces, axis=0))
        hidden = jax.nn.gelu(whole, approximate=True).astype(BF16)
        loads[n, 3].wait()
        result = (after + dot(hidden, wdown[n])).astype(BF16)
        if n == layers - 1:
            out_ref[...] = result
        wide = result.astype(F32)

    for n in range(layers):
        for which in range(2):
            for slot, step in enumerate(STEPS):
                when_to(step, lambda slot=slot: remote(n, which, slot).wait_send())


def on_device(n_lat, n_lon, stream, gains, w_qkv, table, w_out, w_up, conv, w_down):
    rows, cols, width = stream.shape
    layers, heads = table.shape[:2]
    hid = w_up.shape[2]
    vmem = pl.BlockSpec(memory_space=pltpu.VMEM)
    anywhere = pl.BlockSpec(memory_space=pl.ANY)
    result = pl.pallas_call(
        functools.partial(kernel, n_lat, n_lon),
        out_shape=jax.ShapeDtypeStruct((rows * cols, width), BF16),
        in_specs=[vmem] * 4 + [anywhere] * 4,
        out_specs=vmem,
        scratch_shapes=[
            pltpu.VMEM(w_qkv.shape, BF16),
            pltpu.VMEM(w_out.shape, BF16),
            pltpu.VMEM(w_up.shape, BF16),
            pltpu.VMEM(w_down.shape, BF16),
            pltpu.VMEM((layers, 352, 2 * width), BF16),
            pltpu.VMEM((layers, 96, 2 * width), BF16),
            pltpu.VMEM((layers, 96, 2 * width), BF16),
            pltpu.VMEM((layers, 128, 2 * width), BF16),
            pltpu.VMEM((layers, 256, hid), BF16),
            pltpu.VMEM((layers, 32, hid), BF16),
            pltpu.VMEM((layers, 8, 16, hid), BF16),
            pltpu.VMEM((288, hid), F32),
            pltpu.VMEM((256, hid), F32),
            pltpu.VMEM((3, layers * heads, 256), F32),
            pltpu.VMEM((layers, 3, 256, 256), F32),
            pltpu.VMEM((256, width), BF16),
            pltpu.SemaphoreType.DMA((layers, 4)),
            pltpu.SemaphoreType.DMA((2 * layers, 8)),
            pltpu.SemaphoreType.DMA((2 * layers, 8)),
        ],
        compiler_params=pltpu.CompilerParams(
            collective_id=0, has_side_effects=True, vmem_limit_bytes=48 * 1024 * 1024
        ),
    )(
        stream.reshape(rows * cols, width),
        gains,
        table.reshape(layers * heads, *table.shape[2:]),
        conv,
        w_qkv,
        w_out,
        w_up,
        w_down,
    )
    return result.reshape(rows, cols, width)


def solution(mesh):
    sizes = dict(mesh.shape)
    in_specs = (P("lat", "lon", None), P(), P(), P(), P(), P(), P(), P())
    return jax.shard_map(
        functools.partial(on_device, sizes["lat"], sizes["lon"]),
        mesh=mesh,
        in_specs=in_specs,
        out_specs=P("lat", "lon", None),
        check_vma=False,
    )
```

profile of v0, /device:TPU:0, one launch (start us, length us, event | category | flops | bytes accessed | tf_op | source)
XLA Modules:
  0.0 41.2 jit_solution(12303838675788533542)
XLA Ops:
  0.0 0.0 copy-start.6
  0.0 0.0 copy-start.4
  0.0 0.9 %copy.9 = f32[2,4,13,7]{3,2,1,0:T(8,128)S(1)} copy(f32[2,4,13,7]{2,1,3,0:T(4,128)} %param.11) | data formatting | bytes 5824 | tf_op args[3]
  0.9 0.0 copy-done.6
  0.9 0.0 copy-start.5
  1.0 0.0 copy-done.4
  1.0 0.7 %copy-done.5 = f32[2,2,256]{2,1,0:T(2,128)S(1)} copy-done((f32[2,2,256]{2,1,0:T(2,128)S(1)}, f32[2,2,256]{2,1,0:T(2,128)}, u32[]{:S(2)}) %copy-start.5) | copy-done | bytes 4120
  1.6 0.0 copy-start
  1.6 1.1 %copy-done = bf16[2,256,768]{2,1,0:T(8,128)(2,1)S(1)} copy-done((bf16[2,256,768]{2,1,0:T(8,128)(2,1)S(1)}, bf16[2,256,768]{2,1,0:T(8,128)(2,1)}, u32[]{:S(2)}) %copy-start) | copy-done | bytes 786456
  2.8 0.0 copy-start.1
  2.8 1.1 %copy-done.1 = bf16[2,256,768]{2,1,0:T(8,128)(2,1)S(1)} copy-done((bf16[2,256,768]{2,1,0:T(8,128)(2,1)S(1)}, bf16[2,256,768]{2,1,0:T(8,128)(2,1)}, u32[]{:S(2)}) %copy-start.1) | copy-done | bytes 786456
  3.9 0.0 copy-start.2
  3.9 1.1 %copy-done.2 = bf16[2,768,256]{2,1,0:T(8,128)(2,1)S(1)} copy-done((bf16[2,768,256]{2,1,0:T(8,128)(2,1)S(1)}, bf16[2,768,256]{2,1,0:T(8,128)(2,1)}, u32[]{:S(2)}) %copy-start.2) | copy-done | bytes 786456
  5.0 0.0 copy-start.3
  5.0 0.9 %copy-done.3 = bf16[2,256,256]{2,1,0:T(8,128)(2,1)S(1)} copy-done((bf16[2,256,256]{2,1,0:T(8,128)(2,1)S(1)}, bf16[2,256,256]{2,1,0:T(8,128)(2,1)}, u32[]{:S(2)}) %copy-start.3) | copy-done | bytes 262168
  6.0 34.6 %shard_map.82 = bf16[256,256]{1,0:T(8,128)(2,1)S(1)} custom-call(bf16[256,256]{1,0:T(8,128)(2,1)S(1)} %bitcast.5, f32[2,2,256]{2,1,0:T(2,128)S(1)} %copy-done.5, f32[8,13,7]{2,1,0:T(8,128)S(1)} %bitcast.4, f32[2,3,3,768]{3,2,1,0:T(4,128)S(1)} %copy.10.conv_ref, bf16[2,256,768]{2,1,0:T(8,128)(2,1)S(1)} %copy-done, bf16[2,256,256]{2,1,0:T(8,128)(2,1)S(1)} %copy-done.3, ...), custom_call_target="tpu_custom_call" | custom-call | tf_op jit(solution)/shard_map/pallas_call | solution.py:296
  40.6 0.7 %copy.12 = bf16[16,16,256]{2,1,0:T(8,128)(2,1)} copy(bf16[16,16,256]{2,1,0:T(8,128)(2,1)S(1)} %bitcast.3) | data formatting | bytes 262144
  (1 shorter events, 0.0 us)
Async XLA Ops:
  0.0 0.9 %copy-start.6 = (f32[2,3,3,768]{3,0,2,1:T(2,128)S(1)}, f32[2,3,3,768]{3,0,2,1:T(2,128)}, u32[]{:S(2)}) copy-start(f32[2,3,3,768]{3,0,2,1:T(2,128)} %param.14) | copy-start | bytes 165892
  0.0 1.0 %copy-start.4 = (bf16[16,16,256]{2,1,0:T(8,128)(2,1)S(1)}, bf16[16,16,256]{2,1,0:T(8,128)(2,1)}, u32[]{:S(2)}) copy-start(bf16[16,16,256]{2,1,0:T(8,128)(2,1)} %param.8) | copy-start | bytes 393220
  0.9 0.7 %copy-start.5 = (f32[2,2,256]{2,1,0:T(2,128)S(1)}, f32[2,2,256]{2,1,0:T(2,128)}, u32[]{:S(2)}) copy-start(f32[2,2,256]{2,1,0:T(2,128)} %gains_ref.1) | copy-start | bytes 12292
  1.6 1.1 %copy-start = (bf16[2,256,768]{2,1,0:T(8,128)(2,1)S(1)}, bf16[2,256,768]{2,1,0:T(8,128)(2,1)}, u32[]{:S(2)}) copy-start(bf16[2,256,768]{2,1,0:T(8,128)(2,1)} %wqkv_hbm.1) | copy-start | bytes 2359300
  2.8 1.1 %copy-start.1 = (bf16[2,256,768]{2,1,0:T(8,128)(2,1)S(1)}, bf16[2,256,768]{2,1,0:T(8,128)(2,1)}, u32[]{:S(2)}) copy-start(bf16[2,256,768]{2,1,0:T(8,128)(2,1)} %wup_hbm.1) | copy-start | bytes 2359300
  3.9 1.1 %copy-start.2 = (bf16[2,768,256]{2,1,0:T(8,128)(2,1)S(1)}, bf16[2,768,256]{2,1,0:T(8,128)(2,1)}, u32[]{:S(2)}) copy-start(bf16[2,768,256]{2,1,0:T(8,128)(2,1)} %wdown_hbm.1) | copy-start | bytes 2359300
  5.0 0.9 %copy-start.3 = (bf16[2,256,256]{2,1,0:T(8,128)(2,1)S(1)}, bf16[2,256,256]{2,1,0:T(8,128)(2,1)}, u32[]{:S(2)}) copy-start(bf16[2,256,256]{2,1,0:T(8,128)(2,1)} %wout_hbm.1) | copy-start | bytes 786436
where the time goes:
time: 41.6 us; the launch traced here: 41.2 us
  Pallas kernels  34.6 us (83%)
  local copies, waits for them, and re-layouts  6.6 us (16%)
    pallas_call x1, Pallas kernels, on_device(): pl.pallas_call(functools.partial(kernel, n_lat, n_lon), out_shape=jax.Sha...  34.6 us
    unnamed x17, local copies, waits for them, and re-layouts  6.6 us

commit v1 on v0

--- a/solution.py
+++ b/solution.py
@@ -35,14 +35,14 @@
 
 
 def kernel(
-    n_lat, n_lon, x_ref, gains_ref, table_ref, conv_ref, wqkv_hbm, wout_hbm, wup_hbm, wdown_hbm,
-    out_ref, wqkv, wout, wup, wdown, kvb, left, right, edge, lifted, ledge, halo, lpad, pre, flat,
-    bias, attn, w_sem, send_sem, recv_sem,
+    n_lat, n_lon, x_hbm, gains_hbm, table_hbm, conv_hbm, wqkv_hbm, wout_hbm, wup_hbm, wdown_hbm,
+    out_ref, x_ref, gains_ref, table, conv_ref, wqkv, wout, wup, wdown, kvb, left, right, edge, lifted, ledge, halo, lpad, pre, rows, spread,
+    bias, attn, in_sem, w_sem, send_sem, recv_sem,
 ):
     layers = wqkv.shape[0]
     tokens, width = x_ref.shape
     cols = 16
-    heads = table_ref.shape[0] // layers
+    heads = table.shape[2]
     hid = wup.shape[2]
     lat = lax.axis_index("lat")
     lon = lax.axis_index("lon")
@@ -52,11 +52,19 @@
     first_row = lat * (tokens // cols)
 
     loads = {}
+    firsts = (("x", x_hbm, x_ref), ("gains", gains_hbm, gains_ref), ("table", table_hbm, table), ("conv", conv_hbm, conv_ref))
+    for k, (name, src, dst) in enumerate(firsts):
+        loads[name] = pltpu.make_async_copy(src, dst, in_sem.at[k])
+    loads["x"].start()
+    loads["gains"].start()
     for n in range(layers):
         pairs = ((wqkv_hbm, wqkv), (wout_hbm, wout), (wup_hbm, wup), (wdown_hbm, wdown))
         for k, (src, dst) in enumerate(pairs):
             loads[n, k] = pltpu.make_async_copy(src.at[n], dst.at[n], w_sem.at[n, k])
             loads[n, k].start()
+            if n == 0 and k == 0:
+                loads["table"].start()
+                loads["conv"].start()
 
     def target(step):
         return {"lat": lat + step[0], "lon": lax.rem(lon + step[1] + n_lon, n_lon)}
@@ -148,12 +156,9 @@
     head_hot = [hot(head_of == h) for h in range(heads)]
 
     def build_bias():
-        flat[...] = jnp.zeros_like(flat)
-        for a in range(2 * WINDOW - 1):
-            row = table_ref[:, a, :]
-            flat[0, :, 16 * a : 16 * a + 7] = row
-            flat[1, :, 4 * a : 4 * a + 3] = row[:, 0:3]
-            flat[2, :, 4 * a : 4 * a + 4] = row[:, 3:7]
+        for n in range(layers):
+            for b in range(WINDOW):
+                rows[b, heads * n : heads * (n + 1), 0 : 2 * WINDOW - 1] = table[n, b]
         x = iota((16, 256), 1)
         j = iota((16, 256), 0)
         own = x < 160
@@ -169,26 +174,23 @@
                 start = jnp.clip(g - REACH, 0, total_rows - WINDOW)
                 r = first_row + GROUP * group - REACH + p
                 oks.append(col_ok & (r >= start) & (r < start + WINDOW))
+            for half in range(2):
+                at = slice(128 * half, 128 * half + 128)
+                pick = jnp.clip(p[0:8, at] - i + REACH, 0, 2 * WINDOW - 2)
+                for b in range(WINDOW):
+                    spread[b, :, at] = jnp.take_along_axis(rows[b], pick, axis=1)
             for n in range(layers):
                 for h in range(heads):
                     row = n * heads + h
-
-                    def turned(which, shift):
-                        base = pltpu.roll(flat[which, row : row + 1, :], shift % 256, 1)
-                        base = jnp.broadcast_to(base, (16, 256))
-                        return pltpu.roll(base, 0, 1, stride=1, stride_axis=0)
-
-                    value = jnp.where(
-                        own,
-                        turned(0, 16 * i - 51),
-                        jnp.where(
-                            on_left, turned(1, 160 + 4 * i - 7), turned(2, 208 + 4 * i - 24)
-                        ),
-                    )
+                    value = jnp.broadcast_to(spread[0, row : row + 1, :], (16, 256))
+                    for b in range(1, WINDOW):
+                        value = jnp.where(c - j == b - REACH, spread[b, row : row + 1, :], value)
                     at = h * 64 + i * 16
                     for var in range(3):
                         bias[n, var, at : at + 16, :] = jnp.where(oks[var], value, -1000000000.0)
 
+    loads["x"].wait()
+    loads["gains"].wait()
     wide = x_ref[...].astype(F32)
     for n in range(layers):
         norm = normed(wide, gains_ref[n, 0:1, :])
@@ -202,7 +204,9 @@
         send(n, 0)
         query = (dot(norm, wqkv[n, :, :width]).astype(BF16) * (width // heads) ** (-0.5)).astype(BF16)
         if n == 0:
+            loads["table"].wait()
             build_bias()
+            loads["conv"].wait()
         receive(n, 0)
         for group in range(4):
             parts = [
@@ -240,9 +244,9 @@
 
             def column(b):
                 return (
-                    conv_ref[n, 0, b : b + 1, at] * above
-                    + conv_ref[n, 1, b : b + 1, at] * here
-                    + conv_ref[n, 2, b : b + 1, at] * below
+                    conv_ref[0, b, n : n + 1, at] * above
+                    + conv_ref[1, b, n : n + 1, at] * here
+                    + conv_ref[2, b, n : n + 1, at] * below
                 )
 
             pre[:, at] = (
@@ -255,7 +259,7 @@
         got = [halo[n, slot].astype(F32) for slot in range(8)]
 
         def tap(a, b):
-            return conv_ref[n, a, b : b + 1, :]
+            return conv_ref[a, b, n : n + 1, :]
 
         def row_part(a, middle, at_left, at_right):
             back = jnp.where(line == 0, pltpu.roll(at_left, 1, 0), pltpu.roll(middle, 1, 0))
@@ -290,15 +294,21 @@
 def on_device(n_lat, n_lon, stream, gains, w_qkv, table, w_out, w_up, conv, w_down):
     rows, cols, width = stream.shape
     layers, heads = table.shape[:2]
+    table = table.transpose(0, 3, 1, 2)
+    conv = conv.transpose(1, 2, 0, 3)
     hid = w_up.shape[2]
     vmem = pl.BlockSpec(memory_space=pltpu.VMEM)
-    anywhere = pl.BlockSpec(memory_space=pl.ANY)
+    anywhere = pl.BlockSpec(memory_space=pltpu.HBM)
     result = pl.pallas_call(
         functools.partial(kernel, n_lat, n_lon),
         out_shape=jax.ShapeDtypeStruct((rows * cols, width), BF16),
-        in_specs=[vmem] * 4 + [anywhere] * 4,
+        in_specs=[anywhere] * 8,
         out_specs=vmem,
         scratch_shapes=[
+            pltpu.VMEM((rows * cols, width), BF16),
+            pltpu.VMEM(gains.shape, F32),
+            pltpu.VMEM(table.shape, F32),
+            pltpu.VMEM(conv.shape, F32),
             pltpu.VMEM(w_qkv.shape, BF16),
             pltpu.VMEM(w_out.shape, BF16),
             pltpu.VMEM(w_up.shape, BF16),
@@ -312,20 +322,22 @@
             pltpu.VMEM((layers, 8, 16, hid), BF16),
             pltpu.VMEM((288, hid), F32),
             pltpu.VMEM((256, hid), F32),
-            pltpu.VMEM((3, layers * heads, 256), F32),
+            pltpu.VMEM((WINDOW, layers * heads, 128), F32),
+            pltpu.VMEM((WINDOW, layers * heads, 256), F32),
             pltpu.VMEM((layers, 3, 256, 256), F32),
             pltpu.VMEM((256, width), BF16),
+            pltpu.SemaphoreType.DMA((4,)),
             pltpu.SemaphoreType.DMA((layers, 4)),
             pltpu.SemaphoreType.DMA((2 * layers, 8)),
             pltpu.SemaphoreType.DMA((2 * layers, 8)),
         ],
         compiler_params=pltpu.CompilerParams(
-            collective_id=0, has_side_effects=True, vmem_limit_bytes=48 * 1024 * 1024
+            collective_id=0, has_side_effects=True, vmem_limit_bytes=64 * 1024 * 1024
         ),
     )(
         stream.reshape(rows * cols, width),
         gains,
-        table.reshape(layers * heads, *table.shape[2:]),
+        table,
         conv,
         w_qkv,
         w_out,

time: 41.6 us -> 35.5 us (0.85)
  local copies, waits for them, and re-layouts: 6.6 us -> 1.57 us
  Pallas kernels: 34.6 us -> 33.8 us
    unnamed x17 -> x1, local copies, waits for them, and re-layouts: 6.6 us -> 1.57 us
    pallas_call x1, Pallas kernels: 34.6 us -> 33.8 us  [on_device(): pl.pallas_call(functools.partial(kernel, n_lat, n_lon), out_shape=jax.Sha...]
where the time goes in v1:
time: 35.5 us; the launch traced here: 35.3 us
  Pallas kernels  33.8 us (95%)
  local copies, waits for them, and re-layouts  1.57 us (4%)
    pallas_call x1, Pallas kernels, on_device(): pl.pallas_call(functools.partial(kernel, n_lat, n_lon), out_shape=jax.Sha...  33.8 us
    unnamed x1, local copies, waits for them, and re-layouts  1.57 us

profile of v1, /device:TPU:0, one launch (start us, length us, event | category | flops | bytes accessed | tf_op | source)
XLA Modules:
  0.0 35.3 jit_solution(11615540425068684506)
XLA Ops:
  0.0 33.8 %shard_map.82 = bf16[256,256]{1,0:T(8,128)(2,1)} custom-call(bf16[256,256]{1,0:T(8,128)(2,1)} %bitcast.5, f32[2,2,256]{2,1,0:T(2,128)} %gains_hbm.1, f32[2,7,4,13]{3,2,1,0:T(4,128)} %bitcast.7, f32[3,3,2,768]{3,2,1,0:T(2,128)} %bitcast.6, bf16[2,256,768]{2,1,0:T(8,128)(2,1)} %wqkv_hbm.1, bf16[2,256,256]{2,1,0:T(8,128)(2,1)} %wout_hbm.1, ...), custom_call_target="tpu_custom_call" | custom-call | tf_op jit(solution)/shard_map/pallas_call | solution.py:302
  33.8 1.6 %copy.10 = bf16[16,16,256]{2,1,0:T(8,128)(2,1)} copy(bf16[16,16,256]{2,1,0:T(8,128)(2,1)} %bitcast.4) | data formatting | bytes 262144

commit v2 on v1

v2 whole, which is shorter than its diff:
```python
import functools

import jax
import jax.numpy as jnp
from jax import lax
from jax.experimental import pallas as pl
from jax.experimental.pallas import tpu as pltpu
from jax.sharding import PartitionSpec as P

WINDOW = 7
REACH = 3
GROUP = 4
F32 = jnp.float32
BF16 = jnp.bfloat16

LEFT, RIGHT, TOP, BOTTOM, TOP_L, TOP_R, BOT_L, BOT_R = range(8)
STEPS = ((0, 1), (0, -1), (1, 0), (-1, 0), (1, 1), (1, -1), (-1, 1), (-1, -1))


def iota(shape, dim):
    return lax.broadcasted_iota(jnp.int32, shape, dim)


def hot(cond):
    return jnp.where(cond, 1.0, 0.0).astype(BF16)


def dot(a, b):
    return jnp.dot(a, b, preferred_element_type=F32)


def normed(wide, gain):
    scale = lax.rsqrt(jnp.mean(wide * wide, axis=-1, keepdims=True) + 1e-06)
    return (wide * scale * gain).astype(BF16)


def kernel(
    n_lat, n_lon, x_hbm, gains_hbm, table_hbm, conv_hbm, wqkv_hbm, wout_hbm, wup_hbm, wdown_hbm,
    out_ref, gains_ref, table, conv_ref, wqkv, wout, wup, wdown, kvb, near_l, near_r, xb, left, right, edge, lpad, pre, rows, spread,
    bias, row_bias, attn, in_sem, w_sem, send_sem, recv_sem,
):
    layers = wqkv.shape[0]
    tokens, width = x_hbm.shape
    cols = 16
    heads = table.shape[2]
    hid = wup.shape[2]
    lat = lax.axis_index("lat")
    lon = lax.axis_index("lon")
    has_up = lat > 0
    has_down = lat < n_lat - 1
    total_rows = n_lat * (tokens // cols)
    first_row = lat * (tokens // cols)

    loads = {}
    firsts = (("x", x_hbm, xb.at[0, pl.ds(64, 256)]), ("gains", gains_hbm, gains_ref), ("table", table_hbm, table), ("conv", conv_hbm, conv_ref))
    for k, (name, src, dst) in enumerate(firsts):
        loads[name] = pltpu.make_async_copy(src, dst, in_sem.at[k])
    loads["x"].start()
    loads["gains"].start()
    for n in range(layers):
        pairs = ((wqkv_hbm, wqkv), (wout_hbm, wout), (wup_hbm, wup), (wdown_hbm, wdown))
        for k, (src, dst) in enumerate(pairs):
            loads[n, k] = pltpu.make_async_copy(src.at[n], dst.at[n], w_sem.at[n, k])
            loads[n, k].start()
            if n == 0 and k == 0:
                loads["table"].start()
                loads["conv"].start()

    def target(step):
        return {"lat": lat + step[0], "lon": lax.rem(lon + step[1] + n_lon, n_lon)}

    def when_to(step, go):
        if step[0] == 0:
            go()
        else:
            pl.when(has_down if step[0] > 0 else has_up)(go)

    def when_from(step, go):
        when_to((-step[0], -step[1]), go)

    barrier = pltpu.get_barrier_semaphore()
    for step in STEPS:
        when_to(
            step,
            lambda step=step: pl.semaphore_signal(
                barrier, inc=1, device_id=target(step), device_id_type=pl.DeviceIdType.MESH
            ),
        )

    def remote(n, slot):
        own, lo, ro, ed = xb.at[n], left.at[n], right.at[n], edge.at[n]
        src, dst = (
            (ed.at[pl.ds(64, 64)], lo.at[pl.ds(16, 64)]),
            (ed.at[pl.ds(0, 64)], ro.at[pl.ds(16, 64)]),
            (own.at[pl.ds(256, 64)], own.at[pl.ds(0, 64)]),
            (own.at[pl.ds(64, 64)], own.at[pl.ds(320, 64)]),
            (ed.at[pl.ds(112, 16)], lo.at[pl.ds(0, 16)]),
            (ed.at[pl.ds(48, 16)], ro.at[pl.ds(0, 16)]),
            (ed.at[pl.ds(64, 16)], lo.at[pl.ds(80, 16)]),
            (ed.at[pl.ds(0, 16)], ro.at[pl.ds(80, 16)]),
        )[slot]
        return pltpu.make_async_remote_copy(
            src_ref=src,
            dst_ref=dst,
            send_sem=send_sem.at[n, slot],
            recv_sem=recv_sem.at[n, slot],
            device_id=target(STEPS[slot]),
            device_id_type=pl.DeviceIdType.MESH,
        )

    def send(n):
        for slot, step in enumerate(STEPS):
            when_to(step, lambda slot=slot: remote(n, slot).start())

    def receive(n):
        for slot, step in enumerate(STEPS):
            when_from(step, lambda slot=slot: remote(n, slot).wait_recv())

    @pl.when(jnp.logical_not(has_up))
    def _():
        for n in range(layers):
            xb[n, 0:64] = jnp.zeros((64, width), BF16)
            left[n, 0:16] = jnp.zeros((16, width), BF16)
            right[n, 0:16] = jnp.zeros((16, width), BF16)
        attn[320:352] = jnp.zeros((32, width), BF16)

    @pl.when(jnp.logical_not(has_down))
    def _():
        for n in range(layers):
            xb[n, 320:384] = jnp.zeros((64, width), BF16)
            left[n, 80:96] = jnp.zeros((16, width), BF16)
            right[n, 80:96] = jnp.zeros((16, width), BF16)
        attn[352:384] = jnp.zeros((32, width), BF16)

    lpad[0:16] = jnp.zeros((16, hid), F32)
    lpad[272:288] = jnp.zeros((16, hid), F32)

    m, t = iota((128, tokens), 0), iota((128, tokens), 1)
    pick_kv = hot(t == ((m & 63) >> 2) * cols + (m & 3) + jnp.where(m >= 64, cols - 4, 0))
    m, t = iota((128, 320), 0), iota((128, 320), 1)
    e = m & 31
    side = 4 * (4 * (m >> 4) + (m & 3) + 4)
    flank = jnp.where((m & 15) < 4, 128 + side + 3, jnp.where((m & 15) < 8, 224 + side, -1))
    above = jnp.where(e < 16, 48 + e, jnp.where(e == 16, 143, jnp.where(e == 17, 236, -1)))
    below = jnp.where(e < 16, 64 + e, jnp.where(e == 16, 211, jnp.where(e == 17, 304, -1)))
    pick_ring = hot(t == jnp.where(m < 64, flank, jnp.where(m < 96, above, below)))
    m, t = iota((32, 64), 0), iota((32, 64), 1)
    pick_side = hot(t == ((m & 15) >> 2) * 16 + (m & 3) + jnp.where(m < 16, 0, 4))
    t, k = iota((tokens, 64), 0), iota((tokens, 64), 1)
    place = hot(((k & 15) == (t >> 4)) & ((t & 15) == jnp.where(k < 32, 0, cols - 1)))
    head_of = iota((1, width), 1) >> 6
    head_hot = [hot(head_of == h) for h in range(heads)]

    def prepare(pick):
        for at in (0, 128):
            for b in range(WINDOW):
                spread[b, :, at : at + 128] = jnp.take_along_axis(
                    rows[b], pick[:, at : at + 128], axis=1
                )

    def chosen(row, offset):
        value = jnp.broadcast_to(spread[0, row : row + 1, :], offset.shape)
        for b in range(1, WINDOW):
            value = jnp.where(offset == b - REACH, spread[b, row : row + 1, :], value)
        return value

    def build_bias():
        for n in range(layers):
            for b in range(WINDOW):
                rows[b, heads * n : heads * (n + 1), 0 : 2 * WINDOW - 1] = table[n, b]
        x = iota((16, 256), 1)
        j = iota((16, 256), 0)
        own = x < 160
        on_left = x < 208
        y = jnp.where(on_left, x - 160, x - 208)
        p = jnp.where(own, x >> 4, (y >> 2) - 1)
        c = jnp.where(own, x & 15, jnp.where(on_left, (y & 3) - 4, (y & 3) + cols))
        col_ok = (c - j >= -REACH) & (c - j <= REACH)
        for i in range(GROUP):
            oks = []
            for group in (0, 1, 3):
                g = first_row + GROUP * group + i
                start = jnp.clip(g - REACH, 0, total_rows - WINDOW)
                r = first_row + GROUP * group - REACH + p
                oks.append(col_ok & (r >= start) & (r < start + WINDOW))
            prepare(jnp.clip(p[0:8] - i + REACH, 0, 2 * WINDOW - 2))
            for n in range(layers):
                for h in range(heads):
                    value = chosen(n * heads + h, c - j)
                    at = h * 80 + i * 16
                    for var in range(3):
                        bias[n, var, at : at + 16, :] = jnp.where(oks[var], value, -1000000000.0)
        e = iota((16, 256), 0)
        i, j = e & 3, jnp.where(e < 4, -1, cols)
        px, cx = p, c
        col_ok = (cx - j >= -REACH) & (cx - j <= REACH)
        oks = []
        for group in (0, 1, 3):
            g = first_row + GROUP * group + i
            start = jnp.clip(g - REACH, 0, total_rows - WINDOW)
            r = first_row + GROUP * group - REACH + px
            oks.append(col_ok & (r >= start) & (r < start + WINDOW))
        pick = jnp.clip(px - i + REACH, 0, 2 * WINDOW - 2)[0:8]
        for n in range(layers):
            for h in range(heads):
                value = jnp.zeros((8, 256), F32)
                for b in range(WINDOW):
                    source = jnp.broadcast_to(rows[b, n * heads + h : n * heads + h + 1, :], (8, 128))
                    got = [
                        jnp.take_along_axis(source, pick[:, at : at + 128], axis=1)
                        for at in (0, 128)
                    ]
                    value = jnp.where(
                        (cx - j)[0:8] == b - REACH, jnp.concatenate(got, axis=1), value
                    )
                at = h * 80 + 64
                for var in range(3):
                    bias[n, var, at : at + 8, :] = jnp.where(oks[var][0:8], value, -1000000000.0)
                    bias[n, var, at + 8 : at + 16, :] = jnp.zeros((8, 256), F32)
        x, e = iota((32, 256), 1), iota((32, 256), 0)
        j = jnp.where(e < 16, e, jnp.where(e == 16, -1, cols))
        own, on_left = x < 160, x < 208
        y = jnp.where(on_left, x - 160, x - 208)
        c = jnp.where(own, x & 15, jnp.where(on_left, (y & 3) - 4, (y & 3) + cols))
        for k, (here, first_own, first_near) in enumerate(((-1, -4, -4), (16, 10, 8))):
            away = jnp.where(own, first_own + (x >> 4), first_near + (y >> 2)) - here
            ok = (c - j >= -REACH) & (c - j <= REACH) & (away >= -REACH) & (away <= REACH)
            prepare(jnp.clip(away[0:8] + WINDOW - 1, 0, 2 * WINDOW - 2))
            for n in range(layers):
                for h in range(heads):
                    value = chosen(n * heads + h, c - j)
                    row_bias[n, k, h * 32 : h * 32 + 32, :] = jnp.where(ok, value, -1000000000.0)

    def attend(q, near, held, count):
        stacked = jnp.concatenate([q * head_hot[h] for h in range(heads)], axis=0)
        scores = lax.dot_general(
            stacked, near[:, :width], (((1,), (1,)), ((), ())), preferred_element_type=F32
        )
        scores = scores + held
        raised = jnp.exp(scores - jnp.max(scores, axis=-1, keepdims=True))
        weights = (raised * (1.0 / jnp.sum(raised, axis=-1, keepdims=True))).astype(BF16)
        mixed = dot(weights, near[:, width:])
        total = jnp.where(head_of == 0, mixed[0:count], 0.0)
        for h in range(1, heads):
            total = jnp.where(head_of == h, mixed[count * h : count * (h + 1)], total)
        return total.astype(BF16)

    def near_keys(own, side):
        parts = [kvb[own : own + 160, :], near_l[side : side + 48, :], near_r[side : side + 48, :]]
        return jnp.concatenate(parts, axis=0)

    scale = (width // heads) ** (-0.5)
    loads["x"].wait()
    for n in range(layers):
        current = xb[n, 64:320]
        edge[n] = dot(pick_kv, current).astype(BF16)
        if n == 0:
            count = 2 + jnp.where(has_up, 3, 0) + jnp.where(has_down, 3, 0)
            pl.semaphore_wait(barrier, count)
        send(n)
        if n == 0:
            loads["gains"].wait()
        gain = gains_ref[n, 0:1, :]
        wide = current.astype(F32)
        norm = normed(wide, gain)
        loads[n, 0].wait()
        kvb[64:320] = dot(norm, wqkv[n, :, width:]).astype(BF16)
        query = (dot(norm, wqkv[n, :, :width]).astype(BF16) * scale).astype(BF16)
        if n == 0:
            loads["table"].wait()
            build_bias()
            loads["conv"].wait()
        receive(n)
        around = jnp.concatenate([xb[n, 0:64], xb[n, 320:384], left[n], right[n]], axis=0)
        ring = dot(pick_ring, around)
        near = dot(normed(around.astype(F32), gain), wqkv[n, :, width:]).astype(BF16)
        kvb[0:64] = near[0:64]
        kvb[320:384] = near[64:128]
        near_l[...] = near[128:224]
        near_r[...] = near[224:320]
        ring_query = (dot(normed(ring, gain), wqkv[n, :, :width]).astype(BF16) * scale).astype(BF16)
        for group in range(4):
            at = 64 * group
            more = slice(16 * group, 16 * group + 16)
            q = jnp.concatenate([query[at : at + 64], ring_query[more]], axis=0)
            held = bias[n, (0, 1, 1, 2)[group]]
            got = attend(q, near_keys(at + 16, 16 * group), held, 80)
            attn[at : at + 64, :] = got[0:64]
            attn[256 + 16 * group : 272 + 16 * group, :] = got[64:80]

        @pl.when(has_up)
        def _():
            attn[320:352] = attend(ring_query[64:96], near_keys(0, 0), row_bias[n, 0], 32)

        @pl.when(has_down)
        def _():
            attn[352:384] = attend(ring_query[96:128], near_keys(224, 48), row_bias[n, 1], 32)

        loads[n, 1].wait()
        after = jnp.concatenate([wide, ring], axis=0) + dot(attn[...], wout[n])
        norm = normed(after, gains_ref[n, 1:2, :])
        after = after[0:tokens]
        loads[n, 2].wait()
        lift = dot(norm, wup[n]).astype(BF16)
        sides = dot(pick_side, lift[256:320])
        rims = lift[320:384].astype(F32)
        lpad[16:272] = lift[0:tokens].astype(F32)
        col = iota((tokens, 128), 0) & 15
        for ch in range(hid // 128):
            at = slice(128 * ch, 128 * ch + 128)
            above, here, below = lpad[0:256, at], lpad[16:272, at], lpad[32:288, at]

            def column(b):
                return (
                    conv_ref[0, b, n : n + 1, at] * above
                    + conv_ref[1, b, n : n + 1, at] * here
                    + conv_ref[2, b, n : n + 1, at] * below
                )

            pre[:, at] = (
                column(1)
                + jnp.where(col > 0, pltpu.roll(column(0), 1, 0), 0.0)
                + jnp.where(col < cols - 1, pltpu.roll(column(2), tokens - 1, 0), 0.0)
            )
        line = iota((16, hid), 0)

        def tap(a, b):
            return conv_ref[a, b, n : n + 1, :]

        def row_part(a, rim):
            middle = rim[0:16]
            back = jnp.where(line == 0, rim[16:17], pltpu.roll(middle, 1, 0))
            ahead = jnp.where(line == 15, rim[17:18], pltpu.roll(middle, 15, 0))
            return tap(a, 0) * back + tap(a, 1) * middle + tap(a, 2) * ahead

        def col_part(b, values):
            up = jnp.where(line == 0, 0.0, pltpu.roll(values, 1, 0))
            down = jnp.where(line == 15, 0.0, pltpu.roll(values, 15, 0))
            return tap(0, b) * up + tap(1, b) * values + tap(2, b) * down

        pieces = []
        for part in (col_part(0, sides[0:16]), col_part(2, sides[16:32])):
            high = part.astype(BF16)
            pieces += [high, (part - high.astype(F32)).astype(BF16)]
        pre[0:16] += row_part(0, rims[0:32])
        pre[240:256] += row_part(2, rims[32:64])
        whole = pre[...] + dot(place, jnp.concatenate(pieces, axis=0))
        hidden = jax.nn.gelu(whole, approximate=True).astype(BF16)
        loads[n, 3].wait()
        result = (after + dot(hidden, wdown[n])).astype(BF16)
        if n == layers - 1:
            out_ref[...] = result
        else:
            xb[n + 1, 64:320] = result

    for n in range(layers):
        for slot, step in enumerate(STEPS):
            when_to(step, lambda slot=slot: remote(n, slot).wait_send())


def on_device(n_lat, n_lon, stream, gains, w_qkv, table, w_out, w_up, conv, w_down):
    rows, cols, width = stream.shape
    layers, heads = table.shape[:2]
    table = table.transpose(0, 3, 1, 2)
    conv = conv.transpose(1, 2, 0, 3)
    hid = w_up.shape[2]
    vmem = pl.BlockSpec(memory_space=pltpu.VMEM)
    anywhere = pl.BlockSpec(memory_space=pltpu.HBM)
    result = pl.pallas_call(
        functools.partial(kernel, n_lat, n_lon),
        out_shape=jax.ShapeDtypeStruct((rows * cols, width), BF16),
        in_specs=[anywhere] * 8,
        out_specs=vmem,
        scratch_shapes=[
            pltpu.VMEM(gains.shape, F32),
            pltpu.VMEM(table.shape, F32),
            pltpu.VMEM(conv.shape, F32),
            pltpu.VMEM(w_qkv.shape, BF16),
            pltpu.VMEM(w_out.shape, BF16),
            pltpu.VMEM(w_up.shape, BF16),
            pltpu.VMEM(w_down.shape, BF16),
            pltpu.VMEM((384, 2 * width), BF16),
            pltpu.VMEM((96, 2 * width), BF16),
            pltpu.VMEM((96, 2 * width), BF16),
            pltpu.VMEM((layers, 384, width), BF16),
            pltpu.VMEM((layers, 96, width), BF16),
            pltpu.VMEM((layers, 96, width), BF16),
            pltpu.VMEM((layers, 128, width), BF16),
            pltpu.VMEM((288, hid), F32),
            pltpu.VMEM((256, hid), F32),
            pltpu.VMEM((WINDOW, layers * heads, 128), F32),
            pltpu.VMEM((WINDOW, layers * heads, 256), F32),
            pltpu.VMEM((layers, 3, 320, 256), F32),
            pltpu.VMEM((layers, 2, 128, 256), F32),
            pltpu.VMEM((384, width), BF16),
            pltpu.SemaphoreType.DMA((4,)),
            pltpu.SemaphoreType.DMA((layers, 4)),
            pltpu.SemaphoreType.DMA((layers, 8)),
            pltpu.SemaphoreType.DMA((layers, 8)),
        ],
        compiler_params=pltpu.CompilerParams(
            collective_id=0, has_side_effects=True, vmem_limit_bytes=64 * 1024 * 1024
        ),
    )(
        stream.reshape(rows * cols, width),
        gains,
        table,
        conv,
        w_qkv,
        w_out,
        w_up,
        w_down,
    )
    return result.reshape(rows, cols, width)


def solution(mesh):
    sizes = dict(mesh.shape)
    in_specs = (P("lat", "lon", None), P(), P(), P(), P(), P(), P(), P())
    return jax.shard_map(
        functools.partial(on_device, sizes["lat"], sizes["lon"]),
        mesh=mesh,
        in_specs=in_specs,
        out_specs=P("lat", "lon", None),
        check_vma=False,
    )
```

time: 35.5 us -> 26.9 us (0.76)
  Pallas kernels: 33.8 us -> 25.1 us
    pallas_call x1, Pallas kernels: 33.8 us -> 25.1 us  [on_device(): pl.pallas_call(functools.partial(kernel, n_lat, n_lon), out_shape=jax.Sha...]
where the time goes in v2:
time: 26.9 us; the launch traced here: 26.7 us
  Pallas kernels  25.1 us (93%)
  local copies, waits for them, and re-layouts  1.57 us (6%)
    pallas_call x1, Pallas kernels, on_device(): pl.pallas_call(functools.partial(kernel, n_lat, n_lon), out_shape=jax.Sha...  25.1 us
    unnamed x1, local copies, waits for them, and re-layouts  1.57 us

profile of v2, /device:TPU:0, one launch (start us, length us, event | category | flops | bytes accessed | tf_op | source)
XLA Modules:
  0.0 26.7 jit_solution(13720902973874319055)
XLA Ops:
  0.0 25.1 %shard_map.82 = bf16[256,256]{1,0:T(8,128)(2,1)} custom-call(bf16[256,256]{1,0:T(8,128)(2,1)} %bitcast.5, f32[2,2,256]{2,1,0:T(2,128)} %gains_hbm.1, f32[2,7,4,13]{3,2,1,0:T(4,128)} %bitcast.7, f32[3,3,2,768]{3,2,1,0:T(2,128)} %bitcast.6, bf16[2,256,768]{2,1,0:T(8,128)(2,1)} %wqkv_hbm.1, bf16[2,256,256]{2,1,0:T(8,128)(2,1)} %wout_hbm.1, ...), custom_call_target="tpu_custom_call" | custom-call | tf_op jit(solution)/shard_map/pallas_call | solution.py:369
  25.1 1.6 %copy.10 = bf16[16,16,256]{2,1,0:T(8,128)(2,1)} copy(bf16[16,16,256]{2,1,0:T(8,128)(2,1)} %bitcast.4) | data formatting | bytes 262144

commit v3 on v2

--- a/solution.py
+++ b/solution.py
@@ -368,7 +368,7 @@
     anywhere = pl.BlockSpec(memory_space=pltpu.HBM)
     result = pl.pallas_call(
         functools.partial(kernel, n_lat, n_lon),
-        out_shape=jax.ShapeDtypeStruct((rows * cols, width), BF16),
+        out_shape=pltpu.VMEM((rows * cols, width), BF16),
         in_specs=[anywhere] * 8,
         out_specs=vmem,
         scratch_shapes=[
@@ -399,7 +399,7 @@
             pltpu.SemaphoreType.DMA((layers, 8)),
         ],
         compiler_params=pltpu.CompilerParams(
-            collective_id=0, has_side_effects=True, vmem_limit_bytes=64 * 1024 * 1024
+            collective_id=0, has_side_effects=True, vmem_limit_bytes=58 * 1024 * 1024
         ),
     )(
         stream.reshape(rows * cols, width),

time: 26.9 us -> 25.3 us (0.941)
  local copies, waits for them, and re-layouts: 1.57 us -> 0.66 us
  Pallas kernels: 25.1 us -> 24.5 us
    unnamed x1, local copies, waits for them, and re-layouts: 1.57 us -> 0.66 us
    pallas_call x1, Pallas kernels: 25.1 us -> 24.5 us  [on_device(): pl.pallas_call(functools.partial(kernel, n_lat, n_lon), out_shape=pltpu.V...]
where the time goes in v3:
time: 25.3 us; the launch traced here: 25.2 us
  Pallas kernels  24.5 us (97%)
  local copies, waits for them, and re-layouts  0.66 us (3%)
    pallas_call x1, Pallas kernels, on_device(): pl.pallas_call(functools.partial(kernel, n_lat, n_lon), out_shape=pltpu.V...  24.5 us
    unnamed x1, local copies, waits for them, and re-layouts  0.66 us

profile of v3, /device:TPU:0, one launch (start us, length us, event | category | flops | bytes accessed | tf_op | source)
XLA Modules:
  0.0 25.2 jit_solution(15285601219761409481)
XLA Ops:
  0.0 24.5 %shard_map.82 = bf16[256,256]{1,0:T(8,128)(2,1)S(1)} custom-call(bf16[256,256]{1,0:T(8,128)(2,1)} %bitcast.5, f32[2,2,256]{2,1,0:T(2,128)} %gains_hbm.1, f32[2,7,4,13]{3,2,1,0:T(4,128)} %bitcast.7, f32[3,3,2,768]{3,2,1,0:T(2,128)} %bitcast.6, bf16[2,256,768]{2,1,0:T(8,128)(2,1)} %wqkv_hbm.1, bf16[2,256,256]{2,1,0:T(8,128)(2,1)} %wout_hbm.1, ...), custom_call_target="tpu_custom_call" | custom-call | tf_op jit(solution)/shard_map/pallas_call | solution.py:369
  24.5 0.7 %copy.10 = bf16[16,16,256]{2,1,0:T(8,128)(2,1)} copy(bf16[16,16,256]{2,1,0:T(8,128)(2,1)S(1)} %bitcast.4) | data formatting | bytes 262144
